TPU v7x, 128 devices: a whole 4x4x4 slice. The times are simulated.
128 devices in a mesh: dp: 8 (over z, core), vocab: 16 (over y, x).
Axes of the slice: x: 4, y: 4, z: 4, core: 2. Of those that a mesh axis runs over, the one named last changes fastest.
Arguments:
- hidden: bfloat16 [12288, 896], P(('dp', 'vocab')), may hold values from -400 to 400
- target_ids: int32 [12288], P('dp'), may hold values from 0 to 151935
- owner: int32 [8, 48], P('dp'), may hold values from 0 to 47, each once within a row
- head: bfloat16 [896, 151936], P(None, 'vocab'), may hold values from -0.1875 to 0.1875
Outputs:
- owned_loss: float32 [384, 32], P(('dp', 'vocab'))
Inputs may be any that keep to these rules, and one draw needn't show every extreme that they name: Each row of owner names every slot once.
All inputs are finite; a program needn't handle non-finite values.
Results may differ from a plain program's by a relative error of at most 0.0003.
Values may be sent and summed in bfloat16 or wider, within the bound.
A program may use at most 128 MiB of HBM per device.

v0:
```python
import math
import jax
import jax.numpy as jnp
from jax import lax
from jax.sharding import PartitionSpec as P


def side_by_side(arrays, axis, split_dim, concat_dim, along):
    ends, at = ([], 0)
    for a in arrays[:-1]:
        at += a.shape[along]
        ends.append(at)
    both = jnp.concatenate(arrays, axis=along)
    return tuple(
        jnp.split(
            lax.all_to_all(both, axis, split_axis=split_dim, concat_axis=concat_dim, tiled=True),
            ends,
            axis=along,
        )
    )


def local(hidden, target_ids, owner, head):
    width = head.shape[1]
    base = lax.axis_index("vocab") * width

    def partials(rows, labels):
        logits = jnp.dot(rows, head, preferred_element_type=jnp.float32)
        peak = jnp.max(logits, axis=1)
        expsum = jnp.sum(jnp.exp(logits - peak[:, None]), axis=1)
        column = lax.broadcasted_iota(jnp.int32, logits.shape, 1)
        picked = jnp.sum(jnp.where(column == (labels - base)[:, None], logits, 0.0), axis=1)
        return jnp.stack((peak, expsum, picked), 0)

    gathered = lax.all_gather(hidden, "vocab", axis=0, tiled=True)
    count = gathered.shape[0]
    step_rows = math.gcd(count, 512)
    split_rows = gathered.reshape(count // step_rows, step_rows, gathered.shape[1])
    split_labels = target_ids.reshape(count // step_rows, step_rows)
    results = lax.map(lambda pair: partials(pair[0], pair[1]), (split_rows, split_labels))
    stats = jnp.transpose(results, (1, 0, 2)).reshape(3, count)
    peak, expsum, picked = (stats[0], stats[1], stats[2])
    seq_group = owner.shape[1]
    length = target_ids.shape[0] // seq_group
    shards = lax.axis_size("vocab")
    own_count = seq_group // shards
    slots_row = owner[0]
    slot_index = lax.broadcasted_iota(jnp.int32, (seq_group, seq_group), 0)
    reorder = (slot_index == slots_row[None, :]).astype(jnp.float32)
    ordered_peak = jnp.dot(
        reorder, peak.reshape(seq_group, length), precision=lax.Precision.HIGHEST
    )
    ordered_sum = jnp.dot(
        reorder, expsum.reshape(seq_group, length), precision=lax.Precision.HIGHEST
    )
    ordered_pick = jnp.dot(
        reorder, picked.reshape(seq_group, length), precision=lax.Precision.HIGHEST
    )
    got_peak, got_sum, got_pick = side_by_side(
        (ordered_peak, ordered_sum, ordered_pick), "vocab", 0, 0, 1
    )
    got_peak = got_peak.reshape(shards, own_count, length)
    got_sum = got_sum.reshape(shards, own_count, length)
    got_pick = got_pick.reshape(shards, own_count, length)
    top = jnp.max(got_peak, axis=0)
    total = jnp.sum(got_sum * jnp.exp(got_peak - top[None]), axis=0)
    return top + jnp.log(total) - jnp.sum(got_pick, axis=0)


def solution(mesh):
    return jax.shard_map(
        local,
        mesh=mesh,
        in_specs=(P(("dp", "vocab"), None), P("dp"), P("dp", None), P(None, "vocab")),
        out_specs=P(("dp", "vocab"), None),
        check_vma=False,
    )
```

profile of v0, /device:TPU:0, one launch (start us, length us, event | category | flops | bytes accessed | tf_op | source)
XLA Modules:
  0.0 162.2 jit_solution(14684987293334065380)
XLA Ops:
  6.5 0.0 all-gather.2.cloned.1.call-start
  6.5 0.7 all-gather.2.cloned.1.call-update
  7.3 0.7 reshape.34
  8.0 50.4 %all-gather.2.cloned.1.call-done = bf16[1536,896]{1,0:T(8,128)(2,1)} async-done(((bf16[96,896]{1,0:T(8,128)(2,1)}), bf16[1536,896]{1,0:T(8,128)(2,1)}) %all-gather.2.cloned.1.call-update) | async-done | bytes 2752528 | tf_op jit(solution)/shard_map/all_gather | solution.py:35
  58.3 0.0 copy-start
  58.3 83.0 %while.10 = (s32[]{:T(128)}, f32[3,3,512]{2,1,0:T(4,128)S(1)}, bf16[3,512,896]{2,1,0:T(8,128)(2,1)}, bf16[896,9496]{0,1:T(8,128)(2,1)}, s32[3,512]{1,0:T(4,128)S(1)}, /*index=5*/s32[]{:T(128)}, s32[]{:T(128)}) while((s32[]{:T(128)}, f32[3,3,512]{2,1,0:T(4,128)S(1)}, bf16[3,512,896]{2,1,0:T(8,128)(2,1)}, bf16[896,9496]{0,1:T(8,128)(2,1)}, ...), condition=%wide.region_4.5_spmd, body=%wide.region_0.4_spmd.sunk | while | flops 8741791744 | bytes 56859224 | solution.py:40
  58.3 17.9 %fusion.21 = (f32[512]{0:T(512)S(1)}, f32[512,9496]{0,1:T(8,128)}) fusion(bf16[896,9496]{0,1:T(8,128)(2,1)} %get-tuple-element.122, bf16[3,512,896]{2,1,0:T(8,128)(2,1)} %get-tuple-element.121, s32[]{:T(128)} %get-tuple-element.112), kind=kOutput, calls=%fused_computation.23.clone.1 | convolution fusion | flops 8717479936 | bytes 37384704 | tf_op jit(solution)/shard_map/while/body/eval_jaxpr/dot_general | solution.py:28
  76.3 9.6 %exponential_reduce_fusion.2 = (f32[512]{0:T(512)S(1)}, f32[512]{0:T(512)S(1)}) fusion(f32[512,9496]{0,1:T(8,128)} %get-tuple-element.101, f32[512]{0:T(512)S(1)} %get-tuple-element.102, s32[512]{0:T(512)S(1)} %bitcast.34), kind=kLoop, calls=%fused_computation.2.clone.1 | loop fusion | flops 24308736 | bytes 19456000 | tf_op jit(solution)/shard_map/while/body/eval_jaxpr/reduce_sum | solution.py:30
  86.0 18.0 %fusion.21 = (f32[512]{0:T(512)S(1)}, f32[512,9496]{0,1:T(8,128)}) fusion(bf16[896,9496]{0,1:T(8,128)(2,1)} %get-tuple-element.122, bf16[3,512,896]{2,1,0:T(8,128)(2,1)} %get-tuple-element.121, s32[]{:T(128)} %get-tuple-element.112), kind=kOutput, calls=%fused_computation.23.clone.1 | convolution fusion | flops 8717479936 | bytes 37384704 | tf_op jit(solution)/shard_map/while/body/eval_jaxpr/dot_general | solution.py:28
  104.0 9.6 %exponential_reduce_fusion.2 = (f32[512]{0:T(512)S(1)}, f32[512]{0:T(512)S(1)}) fusion(f32[512,9496]{0,1:T(8,128)} %get-tuple-element.101, f32[512]{0:T(512)S(1)} %get-tuple-element.102, s32[512]{0:T(512)S(1)} %bitcast.34), kind=kLoop, calls=%fused_computation.2.clone.1 | loop fusion | flops 24308736 | bytes 19456000 | tf_op jit(solution)/shard_map/while/body/eval_jaxpr/reduce_sum | solution.py:30
  113.7 17.9 %fusion.21 = (f32[512]{0:T(512)S(1)}, f32[512,9496]{0,1:T(8,128)}) fusion(bf16[896,9496]{0,1:T(8,128)(2,1)} %get-tuple-element.122, bf16[3,512,896]{2,1,0:T(8,128)(2,1)} %get-tuple-element.121, s32[]{:T(128)} %get-tuple-element.112), kind=kOutput, calls=%fused_computation.23.clone.1 | convolution fusion | flops 8717479936 | bytes 37384704 | tf_op jit(solution)/shard_map/while/body/eval_jaxpr/dot_general | solution.py:28
  131.6 9.6 %exponential_reduce_fusion.2 = (f32[512]{0:T(512)S(1)}, f32[512]{0:T(512)S(1)}) fusion(f32[512,9496]{0,1:T(8,128)} %get-tuple-element.101, f32[512]{0:T(512)S(1)} %get-tuple-element.102, s32[512]{0:T(512)S(1)} %bitcast.34), kind=kLoop, calls=%fused_computation.2.clone.1 | loop fusion | flops 24308736 | bytes 19456000 | tf_op jit(solution)/shard_map/while/body/eval_jaxpr/reduce_sum | solution.py:30
  141.3 0.1 slice_reduce_fusion.2
  141.4 0.1 reshape_squeeze.11
  141.5 0.1 reshape_squeeze.10
  141.5 0.0 copy-done
  141.5 0.2 fusion.5
  141.7 0.2 fusion.6
  141.9 0.1 reshape_squeeze.9
  142.0 0.2 fusion.7
  142.3 0.1 copy.6
  142.4 12.1 %all_to_all.12 = f32[16,3,96]{2,1,0:T(4,128)S(1)} all-to-all(f32[16,3,96]{2,1,0:T(4,128)S(1)} %all_to_all.8), channel_id=1, replica_groups=mesh['dp'=8,'vocab'=16] {'vocab'}, dimensions={0} | all-to-all | bytes 36864 | tf_op jit(solution)/shard_map/all_to_all | solution.py:16
  154.5 0.1 fusion.12
  154.7 0.6 add_subtract_fusion
  (16 shorter events, 0.3 us)
Async XLA Ops:
  6.5 51.8 %all-gather.2.cloned.1.call-start = ((), (), s32[]{:S(2)}) async-start(), calls=%async_computation.1 | async-start | bytes 2924544 | tf_op jit(solution)/shard_map/all_gather | solution.py:35
  58.3 83.2 %copy-start = (s32[1,48]{1,0:T(1,128)S(1)}, s32[1,48]{1,0:T(1,128)}, u32[]{:S(2)}) copy-start(s32[1,48]{1,0:T(1,128)} %param.8) | copy-start | bytes 580
Sparse Core Ops, SparseCore 0:
  9.5 48.8 all-gather.1
where the time goes:
time: 163 us; the launch traced here: 162 us
  matrix products  54.5 us (33%)
  waiting for transfers between devices  51.1 us (31%)
  other arithmetic  29.7 us (18%)
  between operations  13.5 us (8%)
  blocking collectives  12.1 us (7%)
    dot_general x3, matrix products, partials(): logits = jnp.dot(rows, head, preferred_element_type=jnp.float32)  53.9 us
    all_gather x1, waiting for transfers between devices, local(): gathered = lax.all_gather(hidden, 'vocab', axis=0, tiled=True)  50.4 us
    reduce_sum x3, other arithmetic, partials(): expsum = jnp.sum(jnp.exp(logits - peak[:, None]), axis=1)  28.9 us
    all_to_all x1, blocking collectives, side_by_side(): lax.all_to_all(both, axis, split_axis=split_dim, concat_axis=concat_dim,...  12.1 us
  transfers between devices with their start and end apart: 1, of which 1 were waited for; matrix products, arithmetic and copies ran while one was open for 0% of the time, Pallas kernels for 0%

commit v1 on v0

--- a/solution.py
+++ b/solution.py
@@ -32,7 +32,9 @@
         picked = jnp.sum(jnp.where(column == (labels - base)[:, None], logits, 0.0), axis=1)
         return jnp.stack((peak, expsum, picked), 0)
 
-    gathered = lax.all_gather(hidden, "vocab", axis=0, tiled=True)
+    gathered = jnp.concatenate(
+        lax.all_to_all(jnp.stack([hidden] * lax.axis_size("vocab")), "vocab", 0, 0), axis=0
+    )
     count = gathered.shape[0]
     step_rows = math.gcd(count, 512)
     split_rows = gathered.reshape(count // step_rows, step_rows, gathered.shape[1])

time: 163 us -> 147 us (0.902)
  between operations: 13.5 us -> 0.07 us
  waiting for transfers between devices: 51.1 us -> 41 us
  starting transfers between devices: 0.01 us -> 7.15 us
  local copies, waits for them, and re-layouts: 1.24 us -> 3.92 us
    all_gather x1 -> x0, waiting for transfers between devices: 50.4 us -> none  [local(): gathered = lax.all_gather(hidden, 'vocab', axis=0, tiled=True)]
    all_to_all x0 -> x1, waiting for transfers between devices: none -> 41 us  [local(): lax.all_to_all(jnp.stack([hidden] * lax.axis_size('vocab')), 'vocab', 0, 0)]
    all_to_all x0 -> x1, starting transfers between devices: none -> 7.15 us  [local(): lax.all_to_all(jnp.stack([hidden] * lax.axis_size('vocab')), 'vocab', 0, 0)]
    another operation x0 -> x1, local copies, waits for them, and re-layouts: none -> 2.68 us  [local(): jnp.stack([hidden] * lax.axis_size('vocab'))]
where the time goes in v1:
time: 147 us
  matrix products  53.7 us (37%)
  waiting for transfers between devices  41 us (28%)
  other arithmetic  29.7 us (20%)
  blocking collectives  11.3 us (8%)
  starting transfers between devices  7.15 us (5%)
  local copies, waits for them, and re-layouts  3.92 us (3%)
    dot_general x3, matrix products, partials(): logits = jnp.dot(rows, head, preferred_element_type=jnp.float32)  53.1 us
    all_to_all x1, waiting for transfers between devices, local(): lax.all_to_all(jnp.stack([hidden] * lax.axis_size('vocab')), 'vocab', 0, 0)  41 us
    reduce_sum x3, other arithmetic, partials(): expsum = jnp.sum(jnp.exp(logits - peak[:, None]), axis=1)  28.9 us
    all_to_all x1, blocking collectives, side_by_side(): lax.all_to_all(both, axis, split_axis=split_dim, concat_axis=concat_dim,...  11.3 us
    all_to_all x1, starting transfers between devices, local(): lax.all_to_all(jnp.stack([hidden] * lax.axis_size('vocab')), 'vocab', 0, 0)  7.15 us
  transfers between devices with their start and end apart: 1, of which 1 were waited for; matrix products, arithmetic and copies ran while one was open for 0% of the time, Pallas kernels for 0%

profile of v1, /device:TPU:0, one launch (start us, length us, event | category | flops | bytes accessed | tf_op | source)
XLA Modules:
  0.0 146.9 jit_solution(6855226768886785421)
XLA Ops:
  0.0 2.7 %stack.10 = bf16[16,96,896]{2,1,0:T(8,128)(2,1)} broadcast(bf16[96,896]{1,0:T(8,128)(2,1)} %param.6), dimensions={1,2} | broadcast | bytes 2924544 | tf_op jit(solution)/shard_map/stack | solution.py:36
  2.7 7.1 %all-to-all-start = ((bf16[16,96,896]{2,1,0:T(8,128)(2,1)}), bf16[16,96,896]{2,1,0:T(8,128)(2,1)S(1)}, u32[]{:S(2)}, u32[]{:S(2)}) async-start(bf16[16,96,896]{2,1,0:T(8,128)(2,1)} %stack.10), calls=%async_computation | async-start | bytes 5505024 | tf_op jit(solution)/shard_map/all_to_all | solution.py:36
  9.8 0.7 reshape.32
  10.6 41.0 %all-to-all-done = bf16[16,96,896]{2,1,0:T(8,128)(2,1)S(1)} async-done(((bf16[16,96,896]{2,1,0:T(8,128)(2,1)}), bf16[16,96,896]{2,1,0:T(8,128)(2,1)S(1)}, u32[]{:S(2)}, u32[]{:S(2)}) %all-to-all-start) | async-done | bytes 2752544 | tf_op jit(solution)/shard_map/all_to_all | solution.py:36
  51.6 0.0 copy-start
  51.6 82.1 %while.10 = (s32[]{:T(128)}, f32[3,3,512]{2,1,0:T(4,128)S(1)}, bf16[3,512,896]{2,1,0:T(8,128)(2,1)S(1)}, bf16[896,9496]{0,1:T(8,128)(2,1)}, s32[3,512]{1,0:T(4,128)S(1)}, /*index=5*/s32[]{:T(128)}, s32[]{:T(128)}) while((s32[]{:T(128)}, f32[3,3,512]{2,1,0:T(4,128)S(1)}, bf16[3,512,896]{2,1,0:T(8,128)(2,1)S(1)}, bf16[896,9496]{0,1:T(8,128)(2,1)}, ...), condition=%wide.region_4.5_spmd, body=%wide.region_0.4_spmd.sunk | while | flops 8741791744 | bytes 56858716 | solution.py:42
  51.6 17.7 %fusion.21 = (f32[512]{0:T(512)S(1)}, f32[512,9496]{0,1:T(8,128)}) fusion(bf16[896,9496]{0,1:T(8,128)(2,1)} %get-tuple-element.122, bf16[3,512,896]{2,1,0:T(8,128)(2,1)S(1)} %get-tuple-element.121, s32[]{:T(128)} %get-tuple-element.112), kind=kOutput, calls=%fused_computation.23.clone.1 | convolution fusion | flops 8717479936 | bytes 37384196 | tf_op jit(solution)/shard_map/while/body/eval_jaxpr/dot_general | solution.py:28
  69.3 9.6 %exponential_reduce_fusion.2 = (f32[512]{0:T(512)S(1)}, f32[512]{0:T(512)S(1)}) fusion(f32[512,9496]{0,1:T(8,128)} %get-tuple-element.101, f32[512]{0:T(512)S(1)} %get-tuple-element.102, s32[512]{0:T(512)S(1)} %bitcast.35), kind=kLoop, calls=%fused_computation.2.clone.1 | loop fusion | flops 24308736 | bytes 19456000 | tf_op jit(solution)/shard_map/while/body/eval_jaxpr/reduce_sum | solution.py:30
  79.0 17.7 %fusion.21 = (f32[512]{0:T(512)S(1)}, f32[512,9496]{0,1:T(8,128)}) fusion(bf16[896,9496]{0,1:T(8,128)(2,1)} %get-tuple-element.122, bf16[3,512,896]{2,1,0:T(8,128)(2,1)S(1)} %get-tuple-element.121, s32[]{:T(128)} %get-tuple-element.112), kind=kOutput, calls=%fused_computation.23.clone.1 | convolution fusion | flops 8717479936 | bytes 37384196 | tf_op jit(solution)/shard_map/while/body/eval_jaxpr/dot_general | solution.py:28
  96.7 9.6 %exponential_reduce_fusion.2 = (f32[512]{0:T(512)S(1)}, f32[512]{0:T(512)S(1)}) fusion(f32[512,9496]{0,1:T(8,128)} %get-tuple-element.101, f32[512]{0:T(512)S(1)} %get-tuple-element.102, s32[512]{0:T(512)S(1)} %bitcast.35), kind=kLoop, calls=%fused_computation.2.clone.1 | loop fusion | flops 24308736 | bytes 19456000 | tf_op jit(solution)/shard_map/while/body/eval_jaxpr/reduce_sum | solution.py:30
  106.4 17.7 %fusion.21 = (f32[512]{0:T(512)S(1)}, f32[512,9496]{0,1:T(8,128)}) fusion(bf16[896,9496]{0,1:T(8,128)(2,1)} %get-tuple-element.122, bf16[3,512,896]{2,1,0:T(8,128)(2,1)S(1)} %get-tuple-element.121, s32[]{:T(128)} %get-tuple-element.112), kind=kOutput, calls=%fused_computation.23.clone.1 | convolution fusion | flops 8717479936 | bytes 37384196 | tf_op jit(solution)/shard_map/while/body/eval_jaxpr/dot_general | solution.py:28
  124.1 9.6 %exponential_reduce_fusion.2 = (f32[512]{0:T(512)S(1)}, f32[512]{0:T(512)S(1)}) fusion(f32[512,9496]{0,1:T(8,128)} %get-tuple-element.101, f32[512]{0:T(512)S(1)} %get-tuple-element.102, s32[512]{0:T(512)S(1)} %bitcast.35), kind=kLoop, calls=%fused_computation.2.clone.1 | loop fusion | flops 24308736 | bytes 19456000 | tf_op jit(solution)/shard_map/while/body/eval_jaxpr/reduce_sum | solution.py:30
  133.7 0.1 slice_reduce_fusion.2
  133.8 0.1 reshape_squeeze.11
  133.9 0.1 reshape_squeeze.10
  133.9 0.0 copy-done
  133.9 0.2 fusion.5
  134.1 0.2 fusion.6
  134.3 0.1 reshape_squeeze.9
  134.4 0.2 fusion.7
  134.7 0.1 copy.6
  134.8 11.3 %all_to_all.17 = f32[16,3,96]{2,1,0:T(4,128)S(1)} all-to-all(f32[16,3,96]{2,1,0:T(4,128)S(1)} %all_to_all.12), channel_id=1, replica_groups=mesh['dp'=8,'vocab'=16] {'vocab'}, dimensions={0} | all-to-all | bytes 36864 | tf_op jit(solution)/shard_map/all_to_all | solution.py:16
  146.0 0.1 fusion.12
  146.3 0.6 add_subtract_fusion
  (16 shorter events, 0.3 us)
Async XLA Ops:
  2.7 48.9 %all-to-all-start = ((bf16[16,96,896]{2,1,0:T(8,128)(2,1)}), bf16[16,96,896]{2,1,0:T(8,128)(2,1)S(1)}, u32[]{:S(2)}, u32[]{:S(2)}) async-start(bf16[16,96,896]{2,1,0:T(8,128)(2,1)} %stack.10), calls=%async_computation | async-start | bytes 5505024 | tf_op jit(solution)/shard_map/all_to_all | solution.py:36
  51.6 82.4 %copy-start = (s32[1,48]{1,0:T(1,128)S(1)}, s32[1,48]{1,0:T(1,128)}, u32[]{:S(2)}) copy-start(s32[1,48]{1,0:T(1,128)} %param.8) | copy-start | bytes 580
